TPU v7x, 256 devices: a whole 4x4x8 slice. The times are simulated.
256 devices in a mesh: pipe: 2 (over x_hi), dp: 128 (over x_lo, z, y, core).
Axes of the slice: x: 4 (x_hi: 2, x_lo: 2; x = x_hi * 2 + x_lo), y: 4, z: 8, core: 2. Of those that a mesh axis runs over, the one named last changes fastest.
Arguments:
- images: bfloat16 [256, 1024, 384], P('dp'), may hold values from -6 to 6
- dw_kernel: bfloat16 [2, 49, 384], P('pipe'), may hold values from -0.875 to 0.875
- dw_bias: bfloat16 [2, 384], P('pipe'), may hold values from -3 to 3
- norm_gain: bfloat16 [2, 384], P('pipe'), may hold values from 0.5 to 1.5
- norm_bias: bfloat16 [2, 384], P('pipe'), may hold values from -3 to 3
- w_in: bfloat16 [2, 384, 1536], P('pipe'), may hold values from -0.3125 to 0.3125
- b_in: bfloat16 [2, 1536], P('pipe'), may hold values from -3 to 3
- w_out: bfloat16 [2, 1536, 384], P('pipe'), may hold values from -0.15625 to 0.15625
- b_out: bfloat16 [2, 384], P('pipe'), may hold values from -3 to 3
- layer_scale: bfloat16 [2, 384], P('pipe'), may hold values from 0.29882812 to 1
- image_embed: bfloat16 [1024, 1024], P(('pipe', 'dp')), may hold values from -8 to 8
- text_embed: bfloat16 [1024, 1024], P('dp'), may hold values from -8 to 8
Outputs:
- section_out: bfloat16 [2, 256, 1024, 384], P('pipe', 'dp')
- row_lse: float32 [1024], P(('pipe', 'dp'))
- col_lse: float32 [1024], P('dp')
- grad_image: float32 [1024, 1024], P(('pipe', 'dp'))
- grad_text: float32 [1024, 1024], P('dp')
All inputs are finite; a program needn't handle non-finite values.
Results may differ from a plain program's by a relative error of at most 0.0055.
Values may be sent and summed in bfloat16 or wider, within the bound.
A program may use at most 128 MiB of HBM per device.

v0:
```python
import math
import jax
import jax.numpy as jnp
from jax import lax
from jax.sharding import PartitionSpec as P


def passed_along(block, axis, distance):
    devices = range(lax.axis_size(axis))
    route = [(i - distance, i) for i in devices if i - distance in devices]
    return lax.ppermute(block, axis, route)


def combined_all(part, axis, combine):
    gathered = jax.tree.map(lambda a: lax.all_gather(a, axis), part)

    def take(source):
        return jax.tree.map(lambda a: lax.dynamic_index_in_dim(a, source, 0, False), gathered)

    return lax.fori_loop(
        1, lax.axis_size(axis), lambda source, state: combine(state, take(source)), take(0)
    )


def convnext_block(feature, params):
    dw_kernel, dw_bias, norm_gain, norm_bias, w_in, b_in, w_out, b_out, layer_scale = params
    count, positions, channels = feature.shape
    side = math.isqrt(positions)
    width = math.isqrt(dw_kernel.shape[0])
    grid = feature.reshape(count, side, side, channels)
    kernel = dw_kernel.reshape(width, width, 1, channels)
    conv = lax.conv_general_dilated(
        grid,
        kernel,
        (1, 1),
        ((width // 2, width // 2), (width // 2, width // 2)),
        dimension_numbers=("NHWC", "HWIO", "NHWC"),
        feature_group_count=channels,
        preferred_element_type=jnp.float32,
    )
    conv = conv.reshape(count * positions, channels) + dw_bias.astype(jnp.float32)
    center = conv - jnp.mean(conv, axis=1, keepdims=True)
    spread = jnp.mean(center * center, axis=1, keepdims=True)
    normed = (
        center * lax.rsqrt(spread + 1e-06) * norm_gain.astype(jnp.float32)
        + norm_bias.astype(jnp.float32)
    ).astype(jnp.bfloat16)
    hidden = jnp.dot(normed, w_in, preferred_element_type=jnp.float32) + b_in.astype(jnp.float32)
    hidden = jax.nn.gelu(hidden, approximate=False).astype(jnp.bfloat16)
    branch = jnp.dot(hidden, w_out, preferred_element_type=jnp.float32) + b_out.astype(jnp.float32)
    result = (
        feature.reshape(count * positions, channels).astype(jnp.float32)
        + layer_scale.astype(jnp.float32) * branch
    )
    return result.astype(jnp.bfloat16).reshape(count, positions, channels)


def unit_rows(values):
    wide = values.astype(jnp.float32)
    return (wide * lax.rsqrt(jnp.sum(wide * wide, axis=1, keepdims=True) + 1e-06)).astype(
        jnp.bfloat16
    )


def merge_stats(first, second):
    top = jnp.maximum(first[0], second[0])
    return (top, first[1] * jnp.exp(first[0] - top) + second[1] * jnp.exp(second[0] - top))


def local(
    images,
    dw_kernel,
    dw_bias,
    norm_gain,
    norm_bias,
    w_in,
    b_in,
    w_out,
    b_out,
    layer_scale,
    image_embed,
    text_embed,
):
    section = lax.axis_index("pipe")
    sections = lax.axis_size("pipe")
    micro = images.shape[0]
    params = (dw_kernel, dw_bias, norm_gain, norm_bias, w_in, b_in, w_out, b_out, layer_scale)
    own = tuple((p[0] for p in params))

    def tick(step, carry):
        incoming, record = carry
        fresh = lax.dynamic_slice_in_dim(images, jnp.clip(step, 0, micro - 1), 1, 0)
        source = jnp.where(section == 0, fresh, incoming)
        result = convnext_block(source, own)
        slot = step - section
        valid = jnp.logical_and(slot >= 0, slot < micro)
        place = jnp.clip(slot, 0, micro - 1)
        before = lax.dynamic_slice_in_dim(record, place, 1, 0)
        record = lax.dynamic_update_slice_in_dim(record, jnp.where(valid, result, before), place, 0)
        incoming = passed_along(result, "pipe", 1)
        return (incoming, record)

    start_state = (
        jnp.zeros((1,) + images.shape[1:], jnp.bfloat16),
        jnp.zeros(images.shape, jnp.bfloat16),
    )
    finished = lax.fori_loop(0, micro + sections - 1, tick, start_state)
    section_out = finished[1][None]
    image_unit = unit_rows(image_embed)
    text_unit = unit_rows(text_embed)
    rows = image_unit.shape[0]
    shard = text_unit.shape[0]
    groups = lax.axis_size("dp")
    pairs = groups * shard
    all_text = lax.all_gather(text_unit, "dp", axis=0, tiled=True)
    logits = 100.0 * jnp.einsum(
        "re,te->rt", image_unit, all_text, preferred_element_type=jnp.float32
    )
    row_top = jnp.max(logits, axis=1)
    row_lse = row_top + jnp.log(jnp.sum(jnp.exp(logits - row_top[:, None]), axis=1))
    first_row = (section * groups + lax.axis_index("dp")) * rows
    first_text = lax.axis_index("dp") * shard
    col_top = jnp.max(logits, axis=0)
    col_total = jnp.sum(jnp.exp(logits - col_top[None, :]), axis=0)
    merged_top, merged_total = combined_all((col_top, col_total), ("pipe", "dp"), merge_stats)
    col_lse = merged_top + jnp.log(merged_total)
    col_out = lax.dynamic_slice_in_dim(col_lse, first_text, shard, 0)
    row_ids = first_row + lax.iota(jnp.int32, rows)
    col_ids = lax.iota(jnp.int32, pairs)
    paired = (row_ids[:, None] == col_ids[None, :]).astype(jnp.float32)
    dlogits = (
        jnp.exp(logits - row_lse[:, None]) + jnp.exp(logits - col_lse[None, :]) - 2.0 * paired
    ).astype(jnp.bfloat16)
    grad_image = 100.0 * jnp.dot(dlogits, all_text, preferred_element_type=jnp.float32)
    partial_rows = lax.psum_scatter(
        100.0 * jnp.einsum("rt,re->te", dlogits, image_unit, preferred_element_type=jnp.float32),
        "dp",
        scatter_dimension=0,
        tiled=True,
    )
    grad_text = lax.psum(partial_rows, "pipe")
    return (section_out, row_lse, col_out, grad_image, grad_text)


def solution(mesh):
    in_specs = (
        P("dp", None, None),
        P("pipe", None, None),
        P("pipe", None),
        P("pipe", None),
        P("pipe", None),
        P("pipe", None, None),
        P("pipe", None),
        P("pipe", None, None),
        P("pipe", None),
        P("pipe", None),
        P(("pipe", "dp"), None),
        P("dp", None),
    )
    out_specs = (
        P("pipe", "dp", None, None),
        P(("pipe", "dp")),
        P("dp"),
        P(("pipe", "dp"), None),
        P("dp", None),
    )
    return jax.shard_map(local, mesh=mesh, in_specs=in_specs, out_specs=out_specs, check_vma=False)
```

profile of v0, /device:TPU:252, one launch (start us, length us, event | category | flops | bytes accessed | tf_op | source)
XLA Modules:
  0.0 1277.5 jit_solution(10016299459213593791)
XLA Ops:
  8.1 1.4 fusion.51
  10.4 210.1 %all-gather.6.cloned.1.call-done = bf16[1024,1024]{1,0:T(8,128)(2,1)} async-done(((bf16[8,1024]{1,0:T(8,128)(2,1)}), bf16[1024,1024]{1,0:T(8,128)(2,1)}) %all-gather.6.cloned.1.call-update) | async-done | bytes 2097168 | tf_op jit(solution)/shard_map/all_gather | solution.py:115
  220.5 2.9 fusion.56
  224.9 102.5 %all-gather.8.cloned.1.call-done = f32[262144]{0:T(1024)} async-done(((f32[1024]{0:T(1024)}), f32[262144]{0:T(1024)}) %all-gather.8.cloned.1.call-update) | async-done | bytes 1048592 | tf_op jit(solution)/shard_map/all_gather | solution.py:15
  327.5 1.5 reshape.163
  328.9 103.8 %all-gather.10.cloned.1.call-done = f32[262144]{0:T(1024)} async-done(((f32[1024]{0:T(1024)}), f32[262144]{0:T(1024)}) %all-gather.10.cloned.1.call-update) | async-done | bytes 1048592 | tf_op jit(solution)/shard_map/all_gather | solution.py:15
  433.4 1.4 reshape.164
  434.8 15.0 %while.34 = (s32[]{:T(128)}, f32[1024]{0:T(1024)S(1)}, f32[1024]{0:T(1024)S(1)}, f32[256,1024]{1,0:T(8,128)S(1)}, f32[256,1024]{1,0:T(8,128)S(1)}, /*index=5*/s32[]{:T(128)}, s32[]{:T(128)}, s32[]{:T(128)}) while((s32[]{:T(128)}, f32[1024]{0:T(1024)S(1)}, f32[1024]{0:T(1024)S(1)}, f32[256,1024]{1,0:T(8,128)S(1)}, ...), condition=%wide.region_11.12_spmd, body=%wide.region_10.11_spmd.sunk | while | flops 6149 | bytes 41083 | solution.py:20
  449.9 2.8 convolution_multiply_fusion
  454.6 561.9 %reduce-scatter.2.cloned.1.call-done = f32[8,1024]{1,0:T(8,128)} async-done(((f32[1024,1024]{1,0:T(8,128)}), f32[8,1024]{1,0:T(8,128)}) %reduce-scatter.2.cloned.1.call-update) | async-done | bytes 32784 | tf_op jit(solution)/shard_map/reduce_scatter | solution.py:135
  1016.5 9.6 psum.7
  1027.4 243.5 %while.33 = (s32[]{:T(128)}, bf16[1,1024,384]{2,1,0:T(8,128)(2,1)S(1)}, bf16[2,1024,384]{2,1,0:T(8,128)(2,1)}, pred[]{:T(512)}, bf16[2,1024,384]{2,1,0:T(8,128)(...) while((s32[]{:T(128)}, ...), condition=%wide.region_3.4_spmd, body=%wide.region_0.3_spmd.sunk | while | flops 2561720832 | bytes 24583492 | solution.py:107
  1028.8 24.1 %add_reduce_fusion.2 = (f32[32,32]{1,0:T(8,128)S(1)}, f32[1,32,32,384]{3,0,2,1:T(1,128)S(1)}) fusion(f32[384]{0:T(512)S(1)} %convert_element_type.178, bf16[7,7,1,384]{3,2,1,0:T(2,128)(2,1)S(1)} %reshape_squeeze.10, bf16[1,32,32,384]{3,2,1,0:T(8,128)(2,1)S(1)} %bitcast.45), kind=kOutput, calls=%fused_computation.32.clone.1 | convolution fusion | flops 35302400 | bytes 2402560 | tf_op jit(solution)/shard_map/while/body/eval_jaxpr/conv_general_dilated | solution.py:32
  1053.0 15.3 %multiply_reduce_fusion.2 = f32[32,32]{1,0:T(8,128)S(1)} fusion(f32[1,32,32,384]{3,0,2,1:T(1,128)S(1)} %get-tuple-element.609, f32[32,32]{1,0:T(8,128)S(1)} %broadcast_multiply_fusion.2, f32[384]{0:T(512)S(1)} %convert_element_type.178), kind=kLoop, calls=%fused_computation.29.clone.1 | loop fusion | flops 1571840 | bytes 1582592 | tf_op jit(solution)/shard_map/while/body/eval_jaxpr/reduce_sum | solution.py:43
  1068.9 18.4 %select_dynamic-update-slice_fusion.2 = (bf16[2,1024,384]{2,1,0:T(8,128)(2,1)}, bf16[1,1024,384]{2,1,0:T(8,128)(2,1)S(1)}) fusion(bf16[2,1024,384]{2,1,0:T(8,128)(2,1)} %get-tuple-element.642, s32[]{:T(128)S(6)} %min.20, pred[]{:T(512)S(6)} %and.11, f32[384]{0:T(512)S(1)} %convert_element_type.177, bf16[1536,384]{1,0:T(8,128)(2,1)} %get-tuple-element.670, ...), kind=kOutput, calls=%fused_computation.33.clone.1 | convolution fusion | flops 2522087424 | bytes 6300677 | tf_op jit(solution)/shard_map/while/body/eval_jaxpr/dot_general | solution.py:50
  1088.6 20.9 %collective-permute-done = bf16[1,1024,384]{2,1,0:T(8,128)(2,1)S(1)} collective-permute-done((bf16[1,1024,384]{2,1,0:T(8,128)(2,1)S(1)}, bf16[1,1024,384]{2,1,0:T(8,128)(2,1)S(1)}, u32[]{:S(2)}, u32[]{:S(2)}) %collective-permute-start) | collective-permute-done | bytes 786464 | tf_op jit(solution)/shard_map/while/body/eval_jaxpr/ppermute | solution.py:11
  1110.9 24.1 %add_reduce_fusion.2 = (f32[32,32]{1,0:T(8,128)S(1)}, f32[1,32,32,384]{3,0,2,1:T(1,128)S(1)}) fusion(f32[384]{0:T(512)S(1)} %convert_element_type.178, bf16[7,7,1,384]{3,2,1,0:T(2,128)(2,1)S(1)} %reshape_squeeze.10, bf16[1,32,32,384]{3,2,1,0:T(8,128)(2,1)S(1)} %bitcast.45), kind=kOutput, calls=%fused_computation.32.clone.1 | convolution fusion | flops 35302400 | bytes 2402560 | tf_op jit(solution)/shard_map/while/body/eval_jaxpr/conv_general_dilated | solution.py:32
  1135.1 15.3 %multiply_reduce_fusion.2 = f32[32,32]{1,0:T(8,128)S(1)} fusion(f32[1,32,32,384]{3,0,2,1:T(1,128)S(1)} %get-tuple-element.609, f32[32,32]{1,0:T(8,128)S(1)} %broadcast_multiply_fusion.2, f32[384]{0:T(512)S(1)} %convert_element_type.178), kind=kLoop, calls=%fused_computation.29.clone.1 | loop fusion | flops 1571840 | bytes 1582592 | tf_op jit(solution)/shard_map/while/body/eval_jaxpr/reduce_sum | solution.py:43
  1151.0 18.4 %select_dynamic-update-slice_fusion.2 = (bf16[2,1024,384]{2,1,0:T(8,128)(2,1)}, bf16[1,1024,384]{2,1,0:T(8,128)(2,1)S(1)}) fusion(bf16[2,1024,384]{2,1,0:T(8,128)(2,1)} %get-tuple-element.642, s32[]{:T(128)S(6)} %min.20, pred[]{:T(512)S(6)} %and.11, f32[384]{0:T(512)S(1)} %convert_element_type.177, bf16[1536,384]{1,0:T(8,128)(2,1)} %get-tuple-element.670, ...), kind=kOutput, calls=%fused_computation.33.clone.1 | convolution fusion | flops 2522087424 | bytes 6300677 | tf_op jit(solution)/shard_map/while/body/eval_jaxpr/dot_general | solution.py:50
  1170.7 20.0 %collective-permute-done = bf16[1,1024,384]{2,1,0:T(8,128)(2,1)S(1)} collective-permute-done((bf16[1,1024,384]{2,1,0:T(8,128)(2,1)S(1)}, bf16[1,1024,384]{2,1,0:T(8,128)(2,1)S(1)}, u32[]{:S(2)}, u32[]{:S(2)}) %collective-permute-start) | collective-permute-done | bytes 786464 | tf_op jit(solution)/shard_map/while/body/eval_jaxpr/ppermute | solution.py:11
  1192.1 24.1 %add_reduce_fusion.2 = (f32[32,32]{1,0:T(8,128)S(1)}, f32[1,32,32,384]{3,0,2,1:T(1,128)S(1)}) fusion(f32[384]{0:T(512)S(1)} %convert_element_type.178, bf16[7,7,1,384]{3,2,1,0:T(2,128)(2,1)S(1)} %reshape_squeeze.10, bf16[1,32,32,384]{3,2,1,0:T(8,128)(2,1)S(1)} %bitcast.45), kind=kOutput, calls=%fused_computation.32.clone.1 | convolution fusion | flops 35302400 | bytes 2402560 | tf_op jit(solution)/shard_map/while/body/eval_jaxpr/conv_general_dilated | solution.py:32
  1216.2 15.3 %multiply_reduce_fusion.2 = f32[32,32]{1,0:T(8,128)S(1)} fusion(f32[1,32,32,384]{3,0,2,1:T(1,128)S(1)} %get-tuple-element.609, f32[32,32]{1,0:T(8,128)S(1)} %broadcast_multiply_fusion.2, f32[384]{0:T(512)S(1)} %convert_element_type.178), kind=kLoop, calls=%fused_computation.29.clone.1 | loop fusion | flops 1571840 | bytes 1582592 | tf_op jit(solution)/shard_map/while/body/eval_jaxpr/reduce_sum | solution.py:43
  1232.2 18.4 %select_dynamic-update-slice_fusion.2 = (bf16[2,1024,384]{2,1,0:T(8,128)(2,1)}, bf16[1,1024,384]{2,1,0:T(8,128)(2,1)S(1)}) fusion(bf16[2,1024,384]{2,1,0:T(8,128)(2,1)} %get-tuple-element.642, s32[]{:T(128)S(6)} %min.20, pred[]{:T(512)S(6)} %and.11, f32[384]{0:T(512)S(1)} %convert_element_type.177, bf16[1536,384]{1,0:T(8,128)(2,1)} %get-tuple-element.670, ...), kind=kOutput, calls=%fused_computation.33.clone.1 | convolution fusion | flops 2522087424 | bytes 6300677 | tf_op jit(solution)/shard_map/while/body/eval_jaxpr/dot_general | solution.py:50
  1251.9 19.1 %collective-permute-done = bf16[1,1024,384]{2,1,0:T(8,128)(2,1)S(1)} collective-permute-done((bf16[1,1024,384]{2,1,0:T(8,128)(2,1)S(1)}, bf16[1,1024,384]{2,1,0:T(8,128)(2,1)S(1)}, u32[]{:S(2)}, u32[]{:S(2)}) %collective-permute-start) | collective-permute-done | bytes 786464 | tf_op jit(solution)/shard_map/while/body/eval_jaxpr/ppermute | solution.py:11
  (610 shorter events, 23.6 us)
Async XLA Ops:
  7.2 442.7 %copy-start.3 = (bf16[4,1024]{1,0:T(4,128)(2,1)S(1)}, bf16[4,1024]{1,0:T(4,128)(2,1)}, u32[]{:S(2)}) copy-start(bf16[4,1024]{1,0:T(4,128)(2,1)} %param.26) | copy-start | bytes 24580
  7.2 213.3 %all-gather.6.cloned.1.call-start = ((), (), s32[]{:S(2)}) async-start(), calls=%async_computation.1 | async-start | bytes 2113536 | tf_op jit(solution)/shard_map/all_gather | solution.py:115
  9.5 318.0 %all-gather.8.cloned.1.call-start = ((), (), s32[]{:S(2)}) async-start(), calls=%async_computation.3 | async-start | bytes 1052672 | tf_op jit(solution)/shard_map/all_gather | solution.py:15
  223.4 209.3 %all-gather.10.cloned.1.call-start = ((), (), s32[]{:S(2)}) async-start(), calls=%async_computation.4 | async-start | bytes 1052672 | tf_op jit(solution)/shard_map/all_gather | solution.py:15
  224.8 791.7 %reduce-scatter.2.cloned.1.call-start = ((), (), s32[]{:S(2)}) async-start(), calls=%async_computation.2 | async-start | bytes 4227072 | tf_op jit(solution)/shard_map/reduce_scatter | solution.py:135
  224.9 228.6 %copy-start.5 = (f32[4]{0:T(128)}, f32[4]{0:T(128)S(1)}, u32[]{:S(2)}) copy-start(f32[4]{0:T(128)S(1)} %log_add_fusion.1) | copy-start | bytes 52
  327.5 107.3 %slice-start = ((f32[262144]{0:T(1024)}), f32[1024]{0:T(1024)S(1)}, s32[]{:S(2)}) async-start(f32[262144]{0:T(1024)} %all-gather.8.cloned.1.call-done), calls=%async_computation.5 | async-start | bytes 8192 | tf_op jit(solution)/shard_map/jit(dynamic_index_in_dim)/dynamic_slice | solution.py:18
  449.9 2.9 copy-start.6
  449.9 2.9 copy-start.7
  449.9 2.9 copy-start.8
  449.9 2.9 copy-start.9
  449.9 2.9 copy-start.10
  449.9 3.0 copy-start.4
  449.9 3.6 copy-start.1
  452.7 574.7 %copy-start.2 = (bf16[1,49,384]{2,1,0:T(8,128)(2,1)S(1)}, bf16[1,49,384]{2,1,0:T(8,128)(2,1)}, u32[]{:S(2)}) copy-start(bf16[1,49,384]{2,1,0:T(8,128)(2,1)} %param.17) | copy-start | bytes 112900
  1028.8 24.1 %copy-start = (bf16[1,1024,384]{2,1,0:T(8,128)(2,1)}, bf16[1,1024,384]{2,1,0:T(8,128)(2,1)S(1)}, u32[]{:S(2)}) copy-start(bf16[1,1024,384]{2,1,0:T(8,128)(2,1)S(1)} %dynamic-slice_select_fusion.2) | copy-start | bytes 2359300 | tf_op jit(solution)/shard_map/while
  1087.3 22.2 %collective-permute-start = (bf16[1,1024,384]{2,1,0:T(8,128)(2,1)S(1)}, bf16[1,1024,384]{2,1,0:T(8,128)(2,1)S(1)}, u32[]{:S(2)}, u32[]{:S(2)}) collective-permute-start(bf16[1,1024,384]{2,1,0:T(8,128)(2,1)S(1)} %get-tuple-element.611), channel_id=1, source_target_pairs={{0,128},{1,129},{2,130},{3,131},{4,132},{5,133},{6,134},{7,135},{8... | collective-permute-start | bytes 2359304 | tf_op jit(solution)/shard_map/while/body/eval_jaxpr/ppermute | solution.py:11
  1110.9 24.1 %copy-start = (bf16[1,1024,384]{2,1,0:T(8,128)(2,1)}, bf16[1,1024,384]{2,1,0:T(8,128)(2,1)S(1)}, u32[]{:S(2)}) copy-start(bf16[1,1024,384]{2,1,0:T(8,128)(2,1)S(1)} %dynamic-slice_select_fusion.2) | copy-start | bytes 2359300 | tf_op jit(solution)/shard_map/while
  1169.4 21.3 %collective-permute-start = (bf16[1,1024,384]{2,1,0:T(8,128)(2,1)S(1)}, bf16[1,1024,384]{2,1,0:T(8,128)(2,1)S(1)}, u32[]{:S(2)}, u32[]{:S(2)}) collective-permute-start(bf16[1,1024,384]{2,1,0:T(8,128)(2,1)S(1)} %get-tuple-element.611), channel_id=1, source_target_pairs={{0,128},{1,129},{2,130},{3,131},{4,132},{5,133},{6,134},{7,135},{8... | collective-permute-start | bytes 2359304 | tf_op jit(solution)/shard_map/while/body/eval_jaxpr/ppermute | solution.py:11
  1192.0 24.1 %copy-start = (bf16[1,1024,384]{2,1,0:T(8,128)(2,1)}, bf16[1,1024,384]{2,1,0:T(8,128)(2,1)S(1)}, u32[]{:S(2)}) copy-start(bf16[1,1024,384]{2,1,0:T(8,128)(2,1)S(1)} %dynamic-slice_select_fusion.2) | copy-start | bytes 2359300 | tf_op jit(solution)/shard_map/while
  1250.6 20.4 %collective-permute-start = (bf16[1,1024,384]{2,1,0:T(8,128)(2,1)S(1)}, bf16[1,1024,384]{2,1,0:T(8,128)(2,1)S(1)}, u32[]{:S(2)}, u32[]{:S(2)}) collective-permute-start(bf16[1,1024,384]{2,1,0:T(8,128)(2,1)S(1)} %get-tuple-element.611), channel_id=1, source_target_pairs={{0,128},{1,129},{2,130},{3,131},{4,132},{5,133},{6,134},{7,135},{8... | collective-permute-start | bytes 2359304 | tf_op jit(solution)/shard_map/while/body/eval_jaxpr/ppermute | solution.py:11
Sparse Core Ops, SparseCore 0:
  10.5 210.0 all-gather.5
  224.8 102.6 all-gather.7
  331.8 100.9 all-gather.9
  452.8 563.5 reduce-scatter.1
where the time goes:
time: 1280 us
  waiting for transfers between devices  1040 us (81%)
  matrix products  134 us (10%)
  other arithmetic  58.5 us (5%)
  between operations  13.9 us (1%)
    reduce_scatter x1, waiting for transfers between devices, local(): lax.psum_scatter(100.0 * jnp.einsum('rt,re->te', dlogits, image_unit, pre...  562 us
    all_gather x1, waiting for transfers between devices, local(): all_text = lax.all_gather(text_unit, 'dp', axis=0, tiled=True)  210 us
    all_gather x2, waiting for transfers between devices, combined_all(): gathered = jax.tree.map(lambda a: lax.all_gather(a, axis), part)  206 us
    conv_general_dilated x3, matrix products, convnext_block(): lax.conv_general_dilated(grid, kernel, (1, 1), ((width // 2, width // 2),...  72.2 us
    ppermute x3, waiting for transfers between devices, passed_along(): return lax.ppermute(block, axis, route)  60 us
    dot_general x3, matrix products, convnext_block(): jnp.dot(hidden, w_out, preferred_element_type=jnp.float32)  55.2 us
    reduce_sum x3, other arithmetic, convnext_block(): spread = jnp.mean(center * center, axis=1, keepdims=True)  46 us
  transfers between devices with their start and end apart: 7, of which 7 were waited for; matrix products, arithmetic and copies ran while one was open for 0% of the time, Pallas kernels for 0%

commit v1 on v0

--- a/solution.py
+++ b/solution.py
@@ -112,7 +112,9 @@
     shard = text_unit.shape[0]
     groups = lax.axis_size("dp")
     pairs = groups * shard
-    all_text = lax.all_gather(text_unit, "dp", axis=0, tiled=True)
+    all_text = jnp.concatenate(
+        lax.all_to_all(jnp.stack([text_unit] * lax.axis_size("dp")), "dp", 0, 0), axis=0
+    )
     logits = 100.0 * jnp.einsum(
         "re,te->rt", image_unit, all_text, preferred_element_type=jnp.float32
     )

time: 1280 us -> 1330 us (1.039); the launches traced: 1280 us -> 1310 us
  local copies, waits for them, and re-layouts: 10.3 us -> 206 us
  waiting for transfers between devices: 1040 us -> 875 us
    all_gather x1 -> x0, waiting for transfers between devices: 210 us -> none  [local(): all_text = lax.all_gather(text_unit, 'dp', axis=0, tiled=True)]
    dynamic_slice x258, local copies, waits for them, and re-layouts: 4.44 us -> 197 us  [take(): lax.dynamic_index_in_dim(a, source, 0, False)]
    all_to_all x0 -> x1, waiting for transfers between devices: none -> 48.6 us  [local(): lax.all_to_all(jnp.stack([text_unit] * lax.axis_size('dp')), 'dp', 0, 0)]
where the time goes in v1:
time: 1330 us; the launch traced here: 1310 us
  waiting for transfers between devices  875 us (66%)
  local copies, waits for them, and re-layouts  206 us (15%)
  matrix products  131 us (10%)
  other arithmetic  56.7 us (4%)
  starting transfers between devices  14.4 us (1%)
  between operations  13.9 us (1%)
    reduce_scatter x1, waiting for transfers between devices, local(): lax.psum_scatter(100.0 * jnp.einsum('rt,re->te', dlogits, image_unit, pre...  562 us
    all_gather x2, waiting for transfers between devices, combined_all(): gathered = jax.tree.map(lambda a: lax.all_gather(a, axis), part)  204 us
    dynamic_slice x258, local copies, waits for them, and re-layouts, take(): lax.dynamic_index_in_dim(a, source, 0, False)  197 us
    conv_general_dilated x3, matrix products, convnext_block(): lax.conv_general_dilated(grid, kernel, (1, 1), ((width // 2, width // 2),...  72.2 us
    ppermute x3, waiting for transfers between devices, passed_along(): return lax.ppermute(block, axis, route)  59.9 us
    dot_general x3, matrix products, convnext_block(): jnp.dot(hidden, w_out, preferred_element_type=jnp.float32)  54.5 us
    all_to_all x1, waiting for transfers between devices, local(): lax.all_to_all(jnp.stack([text_unit] * lax.axis_size('dp')), 'dp', 0, 0)  48.6 us
    reduce_sum x3, other arithmetic, convnext_block(): spread = jnp.mean(center * center, axis=1, keepdims=True)  46 us
  transfers between devices with their start and end apart: 7, of which 7 were waited for; matrix products, arithmetic and copies ran while one was open for 0% of the time, Pallas kernels for 0%

profile of v1, /device:TPU:252, one launch (start us, length us, event | category | flops | bytes accessed | tf_op | source)
XLA Modules:
  0.0 1312.0 jit_solution(10209402001055915329)
XLA Ops:
  8.8 1.6 stack.2
  10.4 10.4 all-to-all-start
  21.0 48.6 %all-to-all-done = bf16[128,8,1024]{2,1,0:T(8,128)(2,1)S(1)} async-done(((bf16[128,8,1024]{2,1,0:T(8,128)(2,1)}), bf16[128,8,1024]{2,1,0:T(8,128)(2,1)S(1)}, u32[]{:S(2)}, u32[]{:S(2)}) %all-to-all-start) | async-done | bytes 2097184 | tf_op jit(solution)/shard_map/all_to_all | solution.py:116
  72.0 100.2 %all-gather.7.cloned.1.call-done = f32[262144]{0:T(1024)} async-done(((f32[1024]{0:T(1024)}), f32[262144]{0:T(1024)}) %all-gather.7.cloned.1.call-update) | async-done | bytes 1048592 | tf_op jit(solution)/shard_map/all_gather | solution.py:15
  172.2 1.5 reshape.170
  173.7 103.8 %all-gather.5.cloned.1.call-done = f32[262144]{0:T(1024)} async-done(((f32[1024]{0:T(1024)}), f32[262144]{0:T(1024)}) %all-gather.5.cloned.1.call-update) | async-done | bytes 1048592 | tf_op jit(solution)/shard_map/all_gather | solution.py:15
  277.5 2.4 reshape.169
  280.5 204.5 %while.34 = (s32[]{:T(128)}, f32[1024]{0:T(1024)S(1)}, f32[1024]{0:T(1024)S(1)}, f32[256,1024]{1,0:T(8,128)}, f32[256,1024]{1,0:T(8,128)S(1)}, /*index=5*/s32[]{:T(128)}, s32[]{:T(128)}, s32[]{:T(128)}) while((s32[]{:T(128)}, f32[1024]{0:T(1024)S(1)}, f32[1024]{0:T(1024)S(1)}, f32[256,1024]{1,0:T(8,128)}, f32[256,1024]{1,0:T(8,128)S(1)}, ...), condition=%wide.region_11.12_spmd, body=%wide.region_10.11_spmd.sunk | while | flops 6149 | bytes 41091 | solution.py:20
  485.1 2.8 convolution_multiply_fusion
  489.7 561.9 %reduce-scatter.2.cloned.1.call-done = f32[8,1024]{1,0:T(8,128)} async-done(((f32[1024,1024]{1,0:T(8,128)}), f32[8,1024]{1,0:T(8,128)}) %reduce-scatter.2.cloned.1.call-update) | async-done | bytes 32784 | tf_op jit(solution)/shard_map/reduce_scatter | solution.py:137
  1051.7 9.6 psum.7
  1062.6 242.9 %while.33 = (s32[]{:T(128)}, bf16[1,1024,384]{2,1,0:T(8,128)(2,1)S(1)}, bf16[2,1024,384]{2,1,0:T(8,128)(2,1)}, pred[]{:T(512)}, bf16[2,1024,384]{2,1,0:T(8,128)(...) while((s32[]{:T(128)}, ...), condition=%wide.region_3.4_spmd, body=%wide.region_0.3_spmd.sunk | while | flops 2561720832 | bytes 21437736 | solution.py:107
  1064.1 24.1 %add_reduce_fusion.2 = (f32[32,32]{1,0:T(8,128)S(1)}, f32[1,32,32,384]{3,0,2,1:T(1,128)S(1)}) fusion(f32[384]{0:T(512)S(1)} %convert_element_type.178, bf16[7,7,1,384]{3,2,1,0:T(2,128)(2,1)S(1)} %reshape_squeeze.10, bf16[1,32,32,384]{3,2,1,0:T(8,128)(2,1)S(1)} %bitcast.54), kind=kOutput, calls=%fused_computation.32.clone.1 | convolution fusion | flops 35302400 | bytes 2402560 | tf_op jit(solution)/shard_map/while/body/eval_jaxpr/conv_general_dilated | solution.py:32
  1088.3 15.3 %multiply_reduce_fusion.2 = f32[32,32]{1,0:T(8,128)S(1)} fusion(f32[1,32,32,384]{3,0,2,1:T(1,128)S(1)} %get-tuple-element.609, f32[32,32]{1,0:T(8,128)S(1)} %broadcast_multiply_fusion.2, f32[384]{0:T(512)S(1)} %convert_element_type.178), kind=kLoop, calls=%fused_computation.29.clone.1 | loop fusion | flops 1571840 | bytes 1582592 | tf_op jit(solution)/shard_map/while/body/eval_jaxpr/reduce_sum | solution.py:43
  1104.3 18.2 %select_dynamic-update-slice_fusion.2 = (bf16[2,1024,384]{2,1,0:T(8,128)(2,1)}, bf16[1,1024,384]{2,1,0:T(8,128)(2,1)S(1)}) fusion(bf16[2,1024,384]{2,1,0:T(8,128)(2,1)} %get-tuple-element.642, s32[]{:T(128)S(6)} %min.20, pred[]{:T(512)S(6)} %and.11, f32[384]{0:T(512)S(1)} %convert_element_type.177, bf16[1536,384]{1,0:T(8,128)(2,1)} %get-tuple-element.670, ...), kind=kOutput, calls=%fused_computation.33.clone.1 | convolution fusion | flops 2522087424 | bytes 6300677 | tf_op jit(solution)/shard_map/while/body/eval_jaxpr/dot_general | solution.py:50
  1123.7 20.9 %collective-permute-done = bf16[1,1024,384]{2,1,0:T(8,128)(2,1)S(1)} collective-permute-done((bf16[1,1024,384]{2,1,0:T(8,128)(2,1)S(1)}, bf16[1,1024,384]{2,1,0:T(8,128)(2,1)S(1)}, u32[]{:S(2)}, u32[]{:S(2)}) %collective-permute-start) | collective-permute-done | bytes 786464 | tf_op jit(solution)/shard_map/while/body/eval_jaxpr/ppermute | solution.py:11
  1146.0 24.1 %add_reduce_fusion.2 = (f32[32,32]{1,0:T(8,128)S(1)}, f32[1,32,32,384]{3,0,2,1:T(1,128)S(1)}) fusion(f32[384]{0:T(512)S(1)} %convert_element_type.178, bf16[7,7,1,384]{3,2,1,0:T(2,128)(2,1)S(1)} %reshape_squeeze.10, bf16[1,32,32,384]{3,2,1,0:T(8,128)(2,1)S(1)} %bitcast.54), kind=kOutput, calls=%fused_computation.32.clone.1 | convolution fusion | flops 35302400 | bytes 2402560 | tf_op jit(solution)/shard_map/while/body/eval_jaxpr/conv_general_dilated | solution.py:32
  1170.2 15.3 %multiply_reduce_fusion.2 = f32[32,32]{1,0:T(8,128)S(1)} fusion(f32[1,32,32,384]{3,0,2,1:T(1,128)S(1)} %get-tuple-element.609, f32[32,32]{1,0:T(8,128)S(1)} %broadcast_multiply_fusion.2, f32[384]{0:T(512)S(1)} %convert_element_type.178), kind=kLoop, calls=%fused_computation.29.clone.1 | loop fusion | flops 1571840 | bytes 1582592 | tf_op jit(solution)/shard_map/while/body/eval_jaxpr/reduce_sum | solution.py:43
  1186.1 18.2 %select_dynamic-update-slice_fusion.2 = (bf16[2,1024,384]{2,1,0:T(8,128)(2,1)}, bf16[1,1024,384]{2,1,0:T(8,128)(2,1)S(1)}) fusion(bf16[2,1024,384]{2,1,0:T(8,128)(2,1)} %get-tuple-element.642, s32[]{:T(128)S(6)} %min.20, pred[]{:T(512)S(6)} %and.11, f32[384]{0:T(512)S(1)} %convert_element_type.177, bf16[1536,384]{1,0:T(8,128)(2,1)} %get-tuple-element.670, ...), kind=kOutput, calls=%fused_computation.33.clone.1 | convolution fusion | flops 2522087424 | bytes 6300677 | tf_op jit(solution)/shard_map/while/body/eval_jaxpr/dot_general | solution.py:50
  1205.6 20.0 %collective-permute-done = bf16[1,1024,384]{2,1,0:T(8,128)(2,1)S(1)} collective-permute-done((bf16[1,1024,384]{2,1,0:T(8,128)(2,1)S(1)}, bf16[1,1024,384]{2,1,0:T(8,128)(2,1)S(1)}, u32[]{:S(2)}, u32[]{:S(2)}) %collective-permute-start) | collective-permute-done | bytes 786464 | tf_op jit(solution)/shard_map/while/body/eval_jaxpr/ppermute | solution.py:11
  1226.8 24.1 %add_reduce_fusion.2 = (f32[32,32]{1,0:T(8,128)S(1)}, f32[1,32,32,384]{3,0,2,1:T(1,128)S(1)}) fusion(f32[384]{0:T(512)S(1)} %convert_element_type.178, bf16[7,7,1,384]{3,2,1,0:T(2,128)(2,1)S(1)} %reshape_squeeze.10, bf16[1,32,32,384]{3,2,1,0:T(8,128)(2,1)S(1)} %bitcast.54), kind=kOutput, calls=%fused_computation.32.clone.1 | convolution fusion | flops 35302400 | bytes 2402560 | tf_op jit(solution)/shard_map/while/body/eval_jaxpr/conv_general_dilated | solution.py:32
  1251.0 15.3 %multiply_reduce_fusion.2 = f32[32,32]{1,0:T(8,128)S(1)} fusion(f32[1,32,32,384]{3,0,2,1:T(1,128)S(1)} %get-tuple-element.609, f32[32,32]{1,0:T(8,128)S(1)} %broadcast_multiply_fusion.2, f32[384]{0:T(512)S(1)} %convert_element_type.178), kind=kLoop, calls=%fused_computation.29.clone.1 | loop fusion | flops 1571840 | bytes 1582592 | tf_op jit(solution)/shard_map/while/body/eval_jaxpr/reduce_sum | solution.py:43
  1267.0 18.2 %select_dynamic-update-slice_fusion.2 = (bf16[2,1024,384]{2,1,0:T(8,128)(2,1)}, bf16[1,1024,384]{2,1,0:T(8,128)(2,1)S(1)}) fusion(bf16[2,1024,384]{2,1,0:T(8,128)(2,1)} %get-tuple-element.642, s32[]{:T(128)S(6)} %min.20, pred[]{:T(512)S(6)} %and.11, f32[384]{0:T(512)S(1)} %convert_element_type.177, bf16[1536,384]{1,0:T(8,128)(2,1)} %get-tuple-element.670, ...), kind=kOutput, calls=%fused_computation.33.clone.1 | convolution fusion | flops 2522087424 | bytes 6300677 | tf_op jit(solution)/shard_map/while/body/eval_jaxpr/dot_general | solution.py:50
  1286.4 19.0 %collective-permute-done = bf16[1,1024,384]{2,1,0:T(8,128)(2,1)S(1)} collective-permute-done((bf16[1,1024,384]{2,1,0:T(8,128)(2,1)S(1)}, bf16[1,1024,384]{2,1,0:T(8,128)(2,1)S(1)}, u32[]{:S(2)}, u32[]{:S(2)}) %collective-permute-start) | collective-permute-done | bytes 786464 | tf_op jit(solution)/shard_map/while/body/eval_jaxpr/ppermute | solution.py:11
  (604 shorter events, 217.5 us)
Async XLA Ops:
  7.2 13.7 %copy-start.1 = (bf16[4,1024]{1,0:T(4,128)(2,1)S(1)}, bf16[4,1024]{1,0:T(4,128)(2,1)}, u32[]{:S(2)}) copy-start(bf16[4,1024]{1,0:T(4,128)(2,1)} %param.26) | copy-start | bytes 24580
  10.4 59.3 %all-to-all-start = ((bf16[128,8,1024]{2,1,0:T(8,128)(2,1)}), bf16[128,8,1024]{2,1,0:T(8,128)(2,1)S(1)}, u32[]{:S(2)}, u32[]{:S(2)}) async-start(bf16[128,8,1024]{2,1,0:T(8,128)(2,1)} %stack.2), calls=%async_computation | async-start | bytes 4194304 | tf_op jit(solution)/shard_map/all_to_all | solution.py:116
  20.9 151.4 %all-gather.7.cloned.1.call-start = ((), (), s32[]{:S(2)}) async-start(), calls=%async_computation.4 | async-start | bytes 1052672 | tf_op jit(solution)/shard_map/all_gather | solution.py:15
  70.5 0.8 copy-start.2
  71.2 206.3 %all-gather.5.cloned.1.call-start = ((), (), s32[]{:S(2)}) async-start(), calls=%async_computation.3 | async-start | bytes 1052672 | tf_op jit(solution)/shard_map/all_gather | solution.py:15
  71.9 979.7 %reduce-scatter.2.cloned.1.call-start = ((), (), s32[]{:S(2)}) async-start(), calls=%async_computation.2 | async-start | bytes 4227072 | tf_op jit(solution)/shard_map/reduce_scatter | solution.py:137
  72.0 416.7 %copy-start.4 = (f32[4]{0:T(128)}, f32[4]{0:T(128)S(1)}, u32[]{:S(2)}) copy-start(f32[4]{0:T(128)S(1)} %log_add_fusion.1) | copy-start | bytes 52
  172.2 108.3 %slice-start = ((f32[262144]{0:T(1024)}), f32[1024]{0:T(1024)S(1)}, s32[]{:S(2)}) async-start(f32[262144]{0:T(1024)} %all-gather.7.cloned.1.call-done), calls=%async_computation.5 | async-start | bytes 8192 | tf_op jit(solution)/shard_map/jit(dynamic_index_in_dim)/dynamic_slice | solution.py:18
  485.0 2.9 copy-start.3
  485.1 2.9 copy-start.5
  485.1 2.9 copy-start.6
  485.1 2.9 copy-start.7
  485.1 2.9 copy-start.8
  485.1 3.0 copy-start.9
  487.9 574.7 %copy-start = (bf16[1,49,384]{2,1,0:T(8,128)(2,1)S(1)}, bf16[1,49,384]{2,1,0:T(8,128)(2,1)}, u32[]{:S(2)}) copy-start(bf16[1,49,384]{2,1,0:T(8,128)(2,1)} %param.17) | copy-start | bytes 112900
  1122.4 22.2 %collective-permute-start = (bf16[1,1024,384]{2,1,0:T(8,128)(2,1)S(1)}, bf16[1,1024,384]{2,1,0:T(8,128)(2,1)S(1)}, u32[]{:S(2)}, u32[]{:S(2)}) collective-permute-start(bf16[1,1024,384]{2,1,0:T(8,128)(2,1)S(1)} %get-tuple-element.611), channel_id=1, source_target_pairs={{0,128},{1,129},{2,130},{3,131},{4,132},{5,133},{6,134},{7,135},{8... | collective-permute-start | bytes 2359304 | tf_op jit(solution)/shard_map/while/body/eval_jaxpr/ppermute | solution.py:11
  1204.3 21.3 %collective-permute-start = (bf16[1,1024,384]{2,1,0:T(8,128)(2,1)S(1)}, bf16[1,1024,384]{2,1,0:T(8,128)(2,1)S(1)}, u32[]{:S(2)}, u32[]{:S(2)}) collective-permute-start(bf16[1,1024,384]{2,1,0:T(8,128)(2,1)S(1)} %get-tuple-element.611), channel_id=1, source_target_pairs={{0,128},{1,129},{2,130},{3,131},{4,132},{5,133},{6,134},{7,135},{8... | collective-permute-start | bytes 2359304 | tf_op jit(solution)/shard_map/while/body/eval_jaxpr/ppermute | solution.py:11
  1285.1 20.3 %collective-permute-start = (bf16[1,1024,384]{2,1,0:T(8,128)(2,1)S(1)}, bf16[1,1024,384]{2,1,0:T(8,128)(2,1)S(1)}, u32[]{:S(2)}, u32[]{:S(2)}) collective-permute-start(bf16[1,1024,384]{2,1,0:T(8,128)(2,1)S(1)} %get-tuple-element.611), channel_id=1, source_target_pairs={{0,128},{1,129},{2,130},{3,131},{4,132},{5,133},{6,134},{7,135},{8... | collective-permute-start | bytes 2359304 | tf_op jit(solution)/shard_map/while/body/eval_jaxpr/ppermute | solution.py:11
Sparse Core Ops, SparseCore 0:
  71.3 100.8 all-gather.6
  176.5 100.9 all-gather.4
  488.0 563.5 reduce-scatter.1
